TPU v7x, 32 devices: a whole 2x2x4 slice. The times are simulated.
32 devices in a mesh: dp: 4 (over y, core), ctx: 4 (over z), tsp: 2 (over x).
Axes of the slice: x: 2, y: 2, z: 4, core: 2. Of those that a mesh axis runs over, the one named last changes fastest.
Arguments:
- grad_out: bfloat16 [4, 1024, 8192], P('dp', 'ctx', 'tsp'), may hold values from -6 to 6
- attn_out: bfloat16 [4, 1024, 4096], P('dp', None, 'ctx'), may hold values from -6 to 6
- out_weight: bfloat16 [4096, 8192], P('ctx', 'tsp'), may hold values from -0.0625 to 0.0625
- query: bfloat16 [4, 1024, 4096], P('dp', 'tsp', 'ctx'), may hold values from -128 to 128
- keys: bfloat16 [4, 1024, 512], P('dp'), may hold values from -128 to 128
- values: bfloat16 [4, 1024, 512], P('dp'), may hold values from -6 to 6
- segment_ids: int32 [4, 1024], P('dp'), may hold values from 0 to 7, never falling along the last dimension, each value on 1 to 256 neighbouring positions
- tile_live: int32 [4, 8, 8], P('dp'), may hold values 0 or 1
Outputs:
- grad_query: bfloat16 [4, 1024, 4096], P('dp', 'tsp', 'ctx')
- grad_keys: bfloat16 [4, 1024, 512], P('dp', ('ctx', 'tsp'))
- grad_values: bfloat16 [4, 1024, 512], P('dp', ('ctx', 'tsp'))
- grad_weight: float32 [4096, 8192], P('ctx', 'tsp')
Inputs may be any that keep to these rules, and one draw needn't show every extreme that they name: `segment_ids`: segment numbers never fall along a row and segment 0 is the source document; each segment has 1 to 256 tokens, one exactly that many.
All inputs are finite; a program needn't handle non-finite values. No bound on the sum of `tile_live` on one device may be relied on, other than what follows from the above.
Results may differ from a plain program's by a relative error of at most 0.0058.
Values may be sent and summed in bfloat16 or wider, within the bound.
A program may use at most 128 MiB of HBM per device.

v0:
```python
import math
import jax
import jax.numpy as jnp
from jax import lax
from jax.sharding import PartitionSpec as P

HEADS = 32
KV_HEADS = 4
HEAD_DIM = 128
TILE = 128


def merge_group(tensor_in):
    row_count = tensor_in.shape[0]
    folded = tensor_in.reshape(row_count, KV_HEADS, HEADS // KV_HEADS, HEAD_DIM).sum(axis=2)
    return folded.reshape(row_count, KV_HEADS * HEAD_DIM)


def per_device(grad_out, attn_out, out_weight, query, keys, values, segment_ids, tile_live):
    score_scale = 1.0 / math.sqrt(HEAD_DIM)
    out_all = attn_out[0]
    seq_len = out_all.shape[0]
    feat_width = out_all.shape[1]
    dy_block = lax.all_gather(grad_out, "ctx", axis=1, tiled=True)[0]
    proj_rows = lax.dot_general(
        dy_block, out_weight, (((1,), (1,)), ((), ())), preferred_element_type=jnp.float32
    )
    grad_part = proj_rows
    weight_part = lax.dot_general(
        out_all, dy_block, (((0,), (0,)), ((), ())), preferred_element_type=jnp.float32
    )
    grad_part, weight_part = (grad_part, weight_part)
    grad_weight = lax.psum(weight_part, "dp")
    out_grad = lax.psum_scatter(grad_part, "tsp", scatter_dimension=0, tiled=True).astype(
        jnp.bfloat16
    )
    quarter = out_grad.shape[0]
    row_start = lax.axis_index("tsp") * quarter
    heads_dev = feat_width // HEAD_DIM
    group_size = HEADS // KV_HEADS
    head_ids = lax.axis_index("ctx") * heads_dev + jnp.arange(heads_dev, dtype=jnp.int32)
    kv_ids = head_ids // group_size
    query_pos = row_start + jnp.arange(quarter, dtype=jnp.int32)
    key_pos = jnp.arange(seq_len, dtype=jnp.int32)
    tile_count = seq_len // TILE
    tile_rows = lax.dynamic_slice_in_dim(tile_live[0], row_start // TILE, quarter // TILE, 0)
    tile_mask = (
        jnp.broadcast_to(
            tile_rows[:, None, :, None], (quarter // TILE, TILE, tile_count, TILE)
        ).reshape(quarter, seq_len)
        == 1
    )
    same_tile = query_pos[:, None] // TILE == key_pos[None, :] // TILE
    segments = segment_ids[0]
    query_seg = lax.dynamic_slice_in_dim(segments, row_start, quarter, 0)
    same_doc = (segments[None, :] == query_seg[:, None]) | (segments[None, :] == 0)
    allowed = (tile_mask | same_tile) & same_doc & (key_pos[None, :] <= query_pos[:, None])

    def split_heads(tensor_in):
        return tensor_in.reshape(tensor_in.shape[0], heads_dev, HEAD_DIM).transpose(1, 0, 2)

    query_heads = split_heads(query[0])
    grad_heads = split_heads(out_grad)
    output_heads = split_heads(lax.dynamic_slice_in_dim(out_all, row_start, quarter, 0))
    key_table = keys[0].reshape(seq_len, KV_HEADS, HEAD_DIM)
    value_table = values[0].reshape(seq_len, KV_HEADS, HEAD_DIM)

    def one_head(head_items):
        query_head, grad_head, output_head, kv_index = head_items
        key_head = lax.dynamic_index_in_dim(key_table, kv_index, 1, keepdims=False)
        value_head = lax.dynamic_index_in_dim(value_table, kv_index, 1, keepdims=False)
        scores = (
            lax.dot_general(
                query_head, key_head, (((1,), (1,)), ((), ())), preferred_element_type=jnp.float32
            )
            * score_scale
        )
        scores = jnp.where(allowed, scores, -jnp.inf)
        row_max = jnp.max(scores, axis=1, keepdims=True)
        lse = row_max + jnp.log(jnp.sum(jnp.exp(scores - row_max), axis=1, keepdims=True))
        probs_f = jnp.where(allowed, jnp.exp(scores - lse), 0.0)
        probs = probs_f.astype(jnp.bfloat16)
        value_term = lax.dot_general(
            probs, grad_head, (((0,), (0,)), ((), ())), preferred_element_type=jnp.float32
        )
        dprobs = lax.dot_general(
            grad_head, value_head, (((1,), (1,)), ((), ())), preferred_element_type=jnp.float32
        )
        delta = jnp.sum(
            grad_head.astype(jnp.float32) * output_head.astype(jnp.float32), axis=1, keepdims=True
        )
        dscores = (probs_f * (dprobs - delta)).astype(jnp.bfloat16)
        query_grad = (
            jnp.dot(dscores, key_head, preferred_element_type=jnp.float32) * score_scale
        ).astype(jnp.bfloat16)
        key_term = (
            lax.dot_general(
                dscores, query_head, (((0,), (0,)), ((), ())), preferred_element_type=jnp.float32
            )
            * score_scale
        )
        return (query_grad, key_term, value_term)

    query_grads, key_terms, value_terms = lax.map(
        one_head, (query_heads, grad_heads, output_heads, kv_ids)
    )
    grad_query = query_grads.transpose(1, 0, 2).reshape(quarter, feat_width)
    key_cols = key_terms.transpose(1, 0, 2).reshape(seq_len, feat_width)
    value_cols = value_terms.transpose(1, 0, 2).reshape(seq_len, feat_width)
    key_recv, value_recv = (
        lax.all_to_all(key_cols, "ctx", split_axis=0, concat_axis=1, tiled=True),
        lax.all_to_all(value_cols, "ctx", split_axis=0, concat_axis=1, tiled=True),
    )
    key_part, value_part = (
        lax.psum_scatter(merge_group(key_recv), "tsp", scatter_dimension=0, tiled=True),
        lax.psum_scatter(merge_group(value_recv), "tsp", scatter_dimension=0, tiled=True),
    )
    grad_keys = key_part.astype(jnp.bfloat16)[None]
    grad_values = value_part.astype(jnp.bfloat16)[None]
    return (grad_query[None], grad_keys, grad_values, grad_weight)


def solution(mesh):
    placed = (
        P("dp", "ctx", "tsp"),
        P("dp", None, "ctx"),
        P("ctx", "tsp"),
        P("dp", "tsp", "ctx"),
        P("dp", None, None),
        P("dp", None, None),
        P("dp", None),
        P("dp", None, None),
    )
    return jax.shard_map(
        per_device,
        mesh=mesh,
        in_specs=placed,
        out_specs=(
            P("dp", "tsp", "ctx"),
            P("dp", ("ctx", "tsp"), None),
            P("dp", ("ctx", "tsp"), None),
            P("ctx", "tsp"),
        ),
        check_vma=False,
    )
```

profile of v0, /device:TPU:0, one launch (start us, length us, event | category | flops | bytes accessed | tf_op | source)
XLA Modules:
  0.0 900.4 jit_solution(15618256980744114519)
XLA Ops:
  8.0 154.0 %all-gather.2.cloned.1.call-done = bf16[1,1024,4096]{2,1,0:T(8,128)(2,1)} async-done(((bf16[1,256,4096]{2,1,0:T(8,128)(2,1)}), bf16[1,1024,4096]{2,1,0:T(8,128)(2,1)}) %all-gather.2.cloned.1.call-update) | async-done | bytes 8388624 | tf_op jit(solution)/shard_map/all_gather | solution.py:24
  161.9 15.1 %fusion.38 = f32[1024,1024]{1,0:T(8,128)} fusion(bf16[1024,4096]{1,0:T(8,128)(2,1)} %param.12, bf16[1,1024,4096]{2,1,0:T(8,128)(2,1)} %all-gather.2.cloned.1.call-done), kind=kOutput, calls=%fused_computation.47 | convolution fusion | flops 8589934592 | bytes 20971520 | tf_op jit(solution)/shard_map/dot_general | solution.py:25
  177.2 1.3 copy.66
  178.5 2.4 copy.46
  182.3 2.3 copy.49
  184.7 45.1 %reduce-scatter.4.cloned.1.call-done = f32[512,1024]{1,0:T(8,128)} async-done(((f32[1024,1024]{1,0:T(8,128)}), f32[512,1024]{1,0:T(8,128)}) %reduce-scatter.4.cloned.1.call-update) | async-done | bytes 2097168 | tf_op jit(solution)/shard_map/reduce_scatter | solution.py:34
  229.7 1.7 bitcast_bitcast_fusion
  231.5 129.6 %while.15 = (s32[]{:T(128)}, bf16[8,512,128]{2,1,0:T(8,128)(2,1)}, f32[8,1024,128]{2,1,0:T(8,128)}, f32[8,1024,128]{2,1,0:T(8,128)}, bf16[8,512,128]{1,2,0:T(8,1...) while((s32[]{:T(128)}, bf16[8,512,128]{2,1,0:T(8,128)(2,1)}, ...), condition=%wide.region_5.6_spmd.clone, body=%wide.region_1.5_spmd.clone.sunk | while | flops 689437696 | bytes 16977196 | solution.py:104
  235.4 2.4 fusion.73
  238.3 2.7 multiply_convert_fusion.2
  241.1 2.1 fusion.75
  243.1 2.4 fusion.77
  245.5 2.2 fusion.76
  251.6 2.4 fusion.73
  254.5 2.7 multiply_convert_fusion.2
  257.3 2.1 fusion.75
  259.3 2.4 fusion.77
  261.8 2.2 fusion.76
  267.9 2.4 fusion.73
  270.8 2.7 multiply_convert_fusion.2
  273.5 2.1 fusion.75
  275.6 2.4 fusion.77
  278.0 2.2 fusion.76
  284.1 2.4 fusion.73
  287.0 2.7 multiply_convert_fusion.2
  289.7 2.1 fusion.75
  291.8 2.4 fusion.77
  294.1 2.2 fusion.76
  300.3 2.4 fusion.73
  303.2 2.7 multiply_convert_fusion.2
  305.9 2.1 fusion.75
  308.0 2.4 fusion.77
  310.4 2.2 fusion.76
  316.5 2.4 fusion.73
  319.4 2.7 multiply_convert_fusion.2
  322.1 2.1 fusion.75
  324.2 2.4 fusion.77
  326.5 2.2 fusion.76
  332.7 2.4 fusion.73
  335.6 2.7 multiply_convert_fusion.2
  338.3 2.1 fusion.75
  340.4 2.4 fusion.77
  342.7 2.2 fusion.76
  348.9 2.4 fusion.73
  351.7 2.7 multiply_convert_fusion.2
  354.5 2.1 fusion.75
  356.5 2.4 fusion.77
  358.9 2.2 fusion.76
  361.1 6.6 copy.58
  367.7 4.9 all_to_all.27
  372.6 4.9 all-to-all-start.1
  377.5 6.5 copy.56
  384.0 4.9 all_to_all.24
  388.9 81.9 %all-to-all-done.1 = f32[4,256,1024]{2,1,0:T(8,128)} async-done(((f32[4,256,1024]{2,1,0:T(8,128)}), f32[4,256,1024]{2,1,0:T(8,128)}, u32[]{:S(2)}, u32[]{:S(2)}) %all-to-all-start.1) | async-done | bytes 4194336 | tf_op jit(solution)/shard_map/all_to_all | solution.py:112
  470.8 4.9 all-to-all-start
  475.8 5.1 copy.70
  480.9 3.2 reduce_sum.37
  485.2 83.3 %all-to-all-done = f32[4,256,1024]{2,1,0:T(8,128)} async-done(((f32[4,256,1024]{2,1,0:T(8,128)}), f32[4,256,1024]{2,1,0:T(8,128)}, u32[]{:S(2)}, u32[]{:S(2)}) %all-to-all-start) | async-done | bytes 4194336 | tf_op jit(solution)/shard_map/all_to_all | solution.py:111
  568.5 5.2 copy.69
  573.7 3.2 reduce_sum.36
  578.0 15.0 %fusion.36 = f32[1024,4096]{1,0:T(8,128)} fusion(bf16[1,1024,4096]{2,1,0:T(8,128)(2,1)} %all-gather.2.cloned.1.call-done, bf16[1,1024,1024]{2,1,0:T(8,128)(2,1)S(1)} %copy-done), kind=kOutput, calls=%fused_computation.45 | convolution fusion | flops 8589934592 | bytes 27262976 | tf_op jit(solution)/shard_map/dot_general | solution.py:29
  593.0 1.9 copy.55
  599.7 282.5 %all-reduce.2.cloned.1.call-done = f32[1024,4096]{1,0:T(8,128)} async-done(((f32[1024,4096]{1,0:T(8,128)}), f32[1024,4096]{1,0:T(8,128)}) %all-reduce.2.cloned.1.call-update) | async-done | bytes 16777232 | tf_op jit(solution)/shard_map/psum | solution.py:33
  882.2 11.7 %copy.104 = f32[1024,4096]{1,0:T(8,128)} copy(f32[1024,4096]{1,0:T(8,128)} %all-reduce.2.cloned.1.call-done) | data formatting | bytes 33554432
  (94 shorter events, 29.3 us)
Async XLA Ops:
  7.2 169.9 %copy-start = (bf16[1,1024,1024]{2,1,0:T(8,128)(2,1)S(1)}, bf16[1,1024,1024]{2,1,0:T(8,128)(2,1)}, u32[]{:S(2)}) copy-start(bf16[1,1024,1024]{2,1,0:T(8,128)(2,1)} %param.11) | copy-start | bytes 6291460
  7.2 154.7 %all-gather.2.cloned.1.call-start = ((), (), s32[]{:S(2)}) async-start(), calls=%async_computation.5 | async-start | bytes 10485760 | tf_op jit(solution)/shard_map/all_gather | solution.py:24
  7.9 221.8 %reduce-scatter.4.cloned.1.call-start = ((), (), s32[]{:S(2)}) async-start(), calls=%async_computation.6 | async-start | bytes 6291456 | tf_op jit(solution)/shard_map/reduce_scatter | solution.py:34
  178.5 2.4 copy-start.1
  180.9 3.6 copy-start.3
  180.9 3.7 copy-start.2
  372.6 98.3 %all-to-all-start.1 = ((f32[4,256,1024]{2,1,0:T(8,128)}), f32[4,256,1024]{2,1,0:T(8,128)}, u32[]{:S(2)}, u32[]{:S(2)}) async-start(f32[4,256,1024]{2,1,0:T(8,128)} %all_to_all.27), calls=%async_computation.3 | async-start | bytes 8388608 | tf_op jit(solution)/shard_map/all_to_all | solution.py:112
  470.8 97.7 %all-to-all-start = ((f32[4,256,1024]{2,1,0:T(8,128)}), f32[4,256,1024]{2,1,0:T(8,128)}, u32[]{:S(2)}, u32[]{:S(2)}) async-start(f32[4,256,1024]{2,1,0:T(8,128)} %all_to_all.24), calls=%async_computation.1 | async-start | bytes 8388608 | tf_op jit(solution)/shard_map/all_to_all | solution.py:111
  475.8 120.4 %reduce-scatter.8.cloned.1.call-start = ((), (), s32[]{:S(2)}) async-start(), calls=%async_computation.8 | async-start | bytes 786432 | tf_op jit(solution)/shard_map/reduce_scatter | solution.py:116
  485.1 112.8 %reduce-scatter.6.cloned.1.call-start = ((), (), s32[]{:S(2)}) async-start(), calls=%async_computation.7 | async-start | bytes 786432 | tf_op jit(solution)/shard_map/reduce_scatter | solution.py:115
  578.0 304.2 %all-reduce.2.cloned.1.call-start = ((), (), s32[]{:S(2)}) async-start(), calls=%async_computation.9 | async-start | bytes 33554432 | tf_op jit(solution)/shard_map/psum | solution.py:33
Sparse Core Ops, SparseCore 0:
  9.6 152.3 all-gather.1
  177.1 52.5 reduce-scatter.3
  485.3 15.0 reduce-scatter.7
  578.1 12.7 reduce-scatter.5
  593.8 288.3 all-reduce.1
where the time goes:
time: 902 us; the launch traced here: 900 us
  waiting for transfers between devices  648 us (72%)
  matrix products  124 us (14%)
  local copies, waits for them, and re-layouts  73.7 us (8%)
  loops' own time  15.8 us (2%)
  other arithmetic  15.5 us (2%)
  between operations  13.9 us (2%)
  starting transfers between devices  10.1 us (1%)
    psum x1, waiting for transfers between devices, per_device(): grad_weight = lax.psum(weight_part, 'dp')  282 us
    all_gather x1, waiting for transfers between devices, per_device(): dy_block = lax.all_gather(grad_out, 'ctx', axis=1, tiled=True)[0]  154 us
    all_to_all x1, waiting for transfers between devices, per_device(): lax.all_to_all(key_cols, 'ctx', split_axis=0, concat_axis=1, tiled=True)  83.3 us
    all_to_all x1, waiting for transfers between devices, per_device(): lax.all_to_all(value_cols, 'ctx', split_axis=0, concat_axis=1, tiled=True)  81.9 us
    reduce_scatter x1, waiting for transfers between devices, per_device(): lax.psum_scatter(grad_part, 'tsp', scatter_dimension=0, tiled=True)  45.1 us
    unnamed x17, local copies, waits for them, and re-layouts  31 us
    dot_general x8, matrix products, one_head(): lax.dot_general(grad_head, value_head, (((1,), (1,)), ((), ())), preferre...  21.9 us
    dot_general x8, matrix products, one_head(): lax.dot_general(probs, grad_head, (((0,), (0,)), ((), ())), preferred_ele...  19.1 us
  transfers between devices with their start and end apart: 7, of which 5 were waited for; matrix products, arithmetic and copies ran while one was open for 6% of the time, Pallas kernels for 0%

commit v1 on v0

--- a/solution.py
+++ b/solution.py
@@ -30,7 +30,7 @@
         out_all, dy_block, (((0,), (0,)), ((), ())), preferred_element_type=jnp.float32
     )
     grad_part, weight_part = (grad_part, weight_part)
-    grad_weight = lax.psum(weight_part, "dp")
+    grad_weight = jnp.sum(lax.all_gather(weight_part, "dp"), axis=0)
     out_grad = lax.psum_scatter(grad_part, "tsp", scatter_dimension=0, tiled=True).astype(
         jnp.bfloat16
     )

time: 902 us -> 1020 us (1.13)
  waiting for transfers between devices: 648 us -> 751 us
  other arithmetic: 15.5 us -> 43.5 us
  local copies, waits for them, and re-layouts: 73.7 us -> 62 us
    all_gather x0 -> x1, waiting for transfers between devices: none -> 386 us  [per_device(): grad_weight = jnp.sum(lax.all_gather(weight_part, 'dp'), axis=0)]
    psum x1 -> x0, waiting for transfers between devices: 282 us -> none  [per_device(): grad_weight = lax.psum(weight_part, 'dp')]
    reduce_sum x0 -> x1, other arithmetic: none -> 27.9 us  [per_device(): grad_weight = jnp.sum(lax.all_gather(weight_part, 'dp'), axis=0)]
    unnamed x17 -> x16, local copies, waits for them, and re-layouts: 31 us -> 19.2 us
  transfers between devices with their start and end apart: 7 -> 7, of which waited for: 5 -> 5; matrix products, arithmetic and copies ran while one was open for 6% -> 5% of each run, Pallas kernels for 0% -> 0%
where the time goes in v1:
time: 1020 us
  waiting for transfers between devices  751 us (74%)
  matrix products  124 us (12%)
  local copies, waits for them, and re-layouts  62 us (6%)
  other arithmetic  43.5 us (4%)
  loops' own time  15.8 us (2%)
  between operations  13.9 us (1%)
    all_gather x1, waiting for transfers between devices, per_device(): grad_weight = jnp.sum(lax.all_gather(weight_part, 'dp'), axis=0)  386 us
    all_gather x1, waiting for transfers between devices, per_device(): dy_block = lax.all_gather(grad_out, 'ctx', axis=1, tiled=True)[0]  154 us
    all_to_all x1, waiting for transfers between devices, per_device(): lax.all_to_all(key_cols, 'ctx', split_axis=0, concat_axis=1, tiled=True)  83.3 us
    all_to_all x1, waiting for transfers between devices, per_device(): lax.all_to_all(value_cols, 'ctx', split_axis=0, concat_axis=1, tiled=True)  81.9 us
    reduce_scatter x1, waiting for transfers between devices, per_device(): lax.psum_scatter(grad_part, 'tsp', scatter_dimension=0, tiled=True)  45.1 us
    reduce_sum x1, other arithmetic, per_device(): grad_weight = jnp.sum(lax.all_gather(weight_part, 'dp'), axis=0)  27.9 us
    dot_general x8, matrix products, one_head(): lax.dot_general(grad_head, value_head, (((1,), (1,)), ((), ())), preferre...  21.9 us
  transfers between devices with their start and end apart: 7, of which 5 were waited for; matrix products, arithmetic and copies ran while one was open for 5% of the time, Pallas kernels for 0%

profile of v1, /device:TPU:0, one launch (start us, length us, event | category | flops | bytes accessed | tf_op | source)
XLA Modules:
  0.0 1020.1 jit_solution(6384269536069524548)
XLA Ops:
  8.0 154.0 %all-gather.4.cloned.1.call-done = bf16[1,1024,4096]{2,1,0:T(8,128)(2,1)} async-done(((bf16[1,256,4096]{2,1,0:T(8,128)(2,1)}), bf16[1,1024,4096]{2,1,0:T(8,128)(2,1)}) %all-gather.4.cloned.1.call-update) | async-done | bytes 8388624 | tf_op jit(solution)/shard_map/all_gather | solution.py:24
  161.9 15.1 %fusion.38 = f32[1024,1024]{1,0:T(8,128)} fusion(bf16[1024,4096]{1,0:T(8,128)(2,1)} %param.12, bf16[1,1024,4096]{2,1,0:T(8,128)(2,1)} %all-gather.4.cloned.1.call-done), kind=kOutput, calls=%fused_computation.47 | convolution fusion | flops 8589934592 | bytes 20971520 | tf_op jit(solution)/shard_map/dot_general | solution.py:25
  177.2 1.3 copy.66
  178.5 2.4 copy.46
  182.3 2.3 copy.49
  184.7 45.1 %reduce-scatter.4.cloned.1.call-done = f32[512,1024]{1,0:T(8,128)} async-done(((f32[1024,1024]{1,0:T(8,128)}), f32[512,1024]{1,0:T(8,128)}) %reduce-scatter.4.cloned.1.call-update) | async-done | bytes 2097168 | tf_op jit(solution)/shard_map/reduce_scatter | solution.py:34
  229.7 1.7 bitcast_bitcast_fusion
  231.5 129.6 %while.15 = (s32[]{:T(128)}, bf16[8,512,128]{2,1,0:T(8,128)(2,1)}, f32[8,1024,128]{2,1,0:T(8,128)}, f32[8,1024,128]{2,1,0:T(8,128)}, bf16[8,512,128]{1,2,0:T(8,1...) while((s32[]{:T(128)}, bf16[8,512,128]{2,1,0:T(8,128)(2,1)}, ...), condition=%wide.region_5.6_spmd.clone, body=%wide.region_1.5_spmd.clone.sunk | while | flops 689437696 | bytes 16977196 | solution.py:104
  235.4 2.4 fusion.73
  238.3 2.7 multiply_convert_fusion.2
  241.1 2.1 fusion.75
  243.1 2.4 fusion.77
  245.5 2.2 fusion.76
  251.6 2.4 fusion.73
  254.5 2.7 multiply_convert_fusion.2
  257.3 2.1 fusion.75
  259.3 2.4 fusion.77
  261.8 2.2 fusion.76
  267.9 2.4 fusion.73
  270.8 2.7 multiply_convert_fusion.2
  273.5 2.1 fusion.75
  275.6 2.4 fusion.77
  278.0 2.2 fusion.76
  284.1 2.4 fusion.73
  287.0 2.7 multiply_convert_fusion.2
  289.7 2.1 fusion.75
  291.8 2.4 fusion.77
  294.1 2.2 fusion.76
  300.3 2.4 fusion.73
  303.2 2.7 multiply_convert_fusion.2
  305.9 2.1 fusion.75
  308.0 2.4 fusion.77
  310.4 2.2 fusion.76
  316.5 2.4 fusion.73
  319.4 2.7 multiply_convert_fusion.2
  322.1 2.1 fusion.75
  324.2 2.4 fusion.77
  326.5 2.2 fusion.76
  332.7 2.4 fusion.73
  335.6 2.7 multiply_convert_fusion.2
  338.3 2.1 fusion.75
  340.4 2.4 fusion.77
  342.7 2.2 fusion.76
  348.9 2.4 fusion.73
  351.7 2.7 multiply_convert_fusion.2
  354.5 2.1 fusion.75
  356.5 2.4 fusion.77
  358.9 2.2 fusion.76
  361.1 6.6 copy.58
  367.7 4.9 all_to_all.27
  372.6 4.9 all-to-all-start.1
  377.5 6.5 copy.56
  384.0 4.9 all_to_all.24
  388.9 81.9 %all-to-all-done.1 = f32[4,256,1024]{2,1,0:T(8,128)} async-done(((f32[4,256,1024]{2,1,0:T(8,128)}), f32[4,256,1024]{2,1,0:T(8,128)}, u32[]{:S(2)}, u32[]{:S(2)}) %all-to-all-start.1) | async-done | bytes 4194336 | tf_op jit(solution)/shard_map/all_to_all | solution.py:112
  470.8 4.9 all-to-all-start
  475.8 5.1 copy.70
  480.9 3.2 reduce_sum.46
  485.2 83.3 %all-to-all-done = f32[4,256,1024]{2,1,0:T(8,128)} async-done(((f32[4,256,1024]{2,1,0:T(8,128)}), f32[4,256,1024]{2,1,0:T(8,128)}, u32[]{:S(2)}, u32[]{:S(2)}) %all-to-all-start) | async-done | bytes 4194336 | tf_op jit(solution)/shard_map/all_to_all | solution.py:111
  568.5 5.2 copy.69
  573.7 3.2 reduce_sum.45
  578.0 15.0 %fusion.36 = f32[1024,4096]{1,0:T(8,128)} fusion(bf16[1,1024,4096]{2,1,0:T(8,128)(2,1)} %all-gather.4.cloned.1.call-done, bf16[1,1024,1024]{2,1,0:T(8,128)(2,1)S(1)} %copy-done), kind=kOutput, calls=%fused_computation.45 | convolution fusion | flops 8589934592 | bytes 27262976 | tf_op jit(solution)/shard_map/dot_general | solution.py:29
  593.0 1.9 copy.55
  599.7 385.9 %all-gather.6.cloned.1.call-done = f32[4096,4096]{1,0:T(8,128)} async-done(((f32[1024,4096]{1,0:T(8,128)}), f32[4096,4096]{1,0:T(8,128)}) %all-gather.6.cloned.1.call-update) | async-done | bytes 67108880 | tf_op jit(solution)/shard_map/all_gather | solution.py:33
  985.6 27.9 %reduce_sum.47 = f32[1024,4096]{1,0:T(8,128)} reduce(f32[4,1024,4096]{2,1,0:T(8,128)} %bitcast.21, f32[]{:T(128)} %constant.90.clone.1), dimensions={0}, to_apply=%region_10.11 | reduce | flops 12582912 | bytes 83886080 | tf_op jit(solution)/shard_map/reduce_sum | solution.py:33
  (94 shorter events, 29.3 us)
Async XLA Ops:
  7.2 169.9 %copy-start = (bf16[1,1024,1024]{2,1,0:T(8,128)(2,1)S(1)}, bf16[1,1024,1024]{2,1,0:T(8,128)(2,1)}, u32[]{:S(2)}) copy-start(bf16[1,1024,1024]{2,1,0:T(8,128)(2,1)} %param.11) | copy-start | bytes 6291460
  7.2 154.7 %all-gather.4.cloned.1.call-start = ((), (), s32[]{:S(2)}) async-start(), calls=%async_computation.5 | async-start | bytes 10485760 | tf_op jit(solution)/shard_map/all_gather | solution.py:24
  7.9 221.8 %reduce-scatter.4.cloned.1.call-start = ((), (), s32[]{:S(2)}) async-start(), calls=%async_computation.6 | async-start | bytes 6291456 | tf_op jit(solution)/shard_map/reduce_scatter | solution.py:34
  178.5 2.4 copy-start.1
  180.9 3.6 copy-start.3
  180.9 3.7 copy-start.2
  372.6 98.3 %all-to-all-start.1 = ((f32[4,256,1024]{2,1,0:T(8,128)}), f32[4,256,1024]{2,1,0:T(8,128)}, u32[]{:S(2)}, u32[]{:S(2)}) async-start(f32[4,256,1024]{2,1,0:T(8,128)} %all_to_all.27), calls=%async_computation.3 | async-start | bytes 8388608 | tf_op jit(solution)/shard_map/all_to_all | solution.py:112
  470.8 97.7 %all-to-all-start = ((f32[4,256,1024]{2,1,0:T(8,128)}), f32[4,256,1024]{2,1,0:T(8,128)}, u32[]{:S(2)}, u32[]{:S(2)}) async-start(f32[4,256,1024]{2,1,0:T(8,128)} %all_to_all.24), calls=%async_computation.1 | async-start | bytes 8388608 | tf_op jit(solution)/shard_map/all_to_all | solution.py:111
  475.8 120.4 %reduce-scatter.8.cloned.1.call-start = ((), (), s32[]{:S(2)}) async-start(), calls=%async_computation.8 | async-start | bytes 786432 | tf_op jit(solution)/shard_map/reduce_scatter | solution.py:116
  485.1 112.8 %reduce-scatter.6.cloned.1.call-start = ((), (), s32[]{:S(2)}) async-start(), calls=%async_computation.7 | async-start | bytes 786432 | tf_op jit(solution)/shard_map/reduce_scatter | solution.py:115
  578.0 407.7 %all-gather.6.cloned.1.call-start = ((), (), s32[]{:S(2)}) async-start(), calls=%async_computation.9 | async-start | bytes 83886080 | tf_op jit(solution)/shard_map/all_gather | solution.py:33
Sparse Core Ops, SparseCore 0:
  9.6 152.3 all-gather.3
  177.1 52.5 reduce-scatter.3
  485.3 15.0 reduce-scatter.7
  578.1 12.7 reduce-scatter.5
  593.1 392.4 all-gather.5
